TPU v7x, 256 devices: a whole 4x4x8 slice. The times are simulated.
256 devices in a mesh: lat: 8 (over z_lo, core), lon: 8 (over z_hi, x), chan: 4 (over y).
Axes of the slice: x: 4, y: 4, z: 8 (z_hi: 2, z_lo: 4; z = z_hi * 4 + z_lo), core: 2. Of those that a mesh axis runs over, the one named last changes fastest.
Arguments:
- queries: bfloat16 [128, 64, 2560], P('lat', 'lon', 'chan'), may hold values from -8 to 8
- keys: bfloat16 [128, 64, 2560], P('lat', 'lon', 'chan'), may hold values from -8 to 8
- values: bfloat16 [128, 64, 2560], P('lat', 'lon', 'chan'), may hold values from -6 to 6
- attn_out: bfloat16 [128, 64, 2560], P('lat', 'lon', 'chan'), may hold values from -6 to 6
- grad_out: bfloat16 [128, 64, 5120], P('lat', 'lon', 'chan'), may hold values from -6 to 6
- w_out: bfloat16 [5120, 2560], P(('lat', 'lon'), 'chan'), may hold values from -0.078125 to 0.078125
- bias_table: float32 [20, 25, 13], P('chan'), may hold values from -5 to 5
- key_mask: int32 [128, 64], replicated, may hold values 0 or 1
Outputs:
- grad_queries: bfloat16 [128, 64, 2560], P('lat', 'lon', 'chan')
- grad_keys: bfloat16 [128, 64, 2560], P('lat', 'lon', 'chan')
- grad_values: bfloat16 [128, 64, 2560], P('lat', 'lon', 'chan')
- grad_wout: float32 [5120, 2560], P(('lat', 'lon'), 'chan')
- grad_table: float32 [20, 25, 13], P('chan')
All inputs are finite; a program needn't handle non-finite values.
Results may differ from a plain program's by a relative error of at most 0.007.
Values may be sent and summed in bfloat16 or wider, within the bound.
No kernel may reach another device: no remote copies, remote signals or barrier semaphores. Data moves between devices by JAX's collectives and lax.ppermute only.
A program may use at most 128 MiB of HBM per device.

v0:
```python
import jax
import jax.numpy as jnp
from jax import lax
from jax.sharding import PartitionSpec as P

HEAD_DIM = 128
WIN = 13


def extended_2(value, sides, width, wrap):
    for axis, dim in sides:
        count, length = (lax.axis_size(axis), value.shape[dim])
        up = [(i, (i + 1) % count) for i in range(count if wrap else count - 1)]
        down = [(j, i) for i, j in up]
        last = lax.slice_in_dim(value, length - width, length, axis=dim)
        leading = lax.slice_in_dim(value, 0, width, axis=dim)
        before = lax.ppermute(last, axis, up)
        after = lax.ppermute(leading, axis, down)
        value = jnp.concatenate([before, value, after], axis=dim)
    return value


def fold_lon(extended, core_width):
    full_width = extended.shape[2]
    reach_cells = (full_width - core_width) // 2
    rim_cells = jnp.concatenate(
        [extended[:, :, :reach_cells], extended[:, :, full_width - reach_cells :]], axis=2
    )
    received = extended_2(rim_cells.astype(jnp.bfloat16), (("lon", 2),), reach_cells, True).astype(
        rim_cells.dtype
    )
    middle = extended[:, :, reach_cells : full_width - reach_cells]
    front_add = jnp.pad(
        received[:, :, :reach_cells], ((0, 0), (0, 0), (0, core_width - reach_cells), (0, 0))
    )
    back_add = jnp.pad(
        received[:, :, 3 * reach_cells :], ((0, 0), (0, 0), (core_width - reach_cells, 0), (0, 0))
    )
    return middle + front_add + back_add


def fold_lat(extended, core_width):
    full_width = extended.shape[1]
    reach_cells = (full_width - core_width) // 2
    rim_cells = jnp.concatenate(
        [extended[:, :reach_cells], extended[:, full_width - reach_cells :]], axis=1
    )
    received = extended_2(rim_cells.astype(jnp.bfloat16), (("lat", 1),), reach_cells, False).astype(
        rim_cells.dtype
    )
    middle = extended[:, reach_cells : full_width - reach_cells]
    front_add = jnp.pad(
        received[:, :reach_cells], ((0, 0), (0, core_width - reach_cells), (0, 0), (0, 0))
    )
    back_add = jnp.pad(
        received[:, 3 * reach_cells :], ((0, 0), (core_width - reach_cells, 0), (0, 0), (0, 0))
    )
    return middle + front_add + back_add


def local(queries, keys, values, attn_out, grad_out, w_out, bias_table, key_mask):
    lat_rows, lon_cols, chan_width = queries.shape
    head_count = bias_table.shape[0]
    reach_cells = WIN // 2
    score_scale = HEAD_DIM ** (-0.5)
    tokens = lat_rows * lon_cols
    ext_rows = lat_rows + 2 * reach_cells
    ext_cols = lon_cols + 2 * reach_cells
    row_block = 4
    key_span = row_block + WIN - 1
    block_count = lat_rows // row_block
    block_rows = row_block * lon_cols
    block_keys = key_span * ext_cols
    offset_rows = 2 * WIN - 1
    low_pad = row_block - 1
    lat_total = lat_rows * lax.axis_size("lat")
    lon_total = lon_cols * lax.axis_size("lon")
    contract_lead = (((0,), (0,)), ((), ()))
    full_grad = lax.all_gather(grad_out, "chan", axis=2, tiled=True).reshape(tokens, -1)
    grad_cols = jnp.transpose(full_grad)
    slab_part = grad_cols
    grad_attn = lax.dot_general(
        slab_part,
        lax.all_gather(w_out, ("lat", "lon"), axis=0, tiled=True),
        contract_lead,
        preferred_element_type=jnp.float32,
    ).astype(jnp.bfloat16)
    kv_pair = jnp.stack([keys, values])
    extended = extended_2(kv_pair, (("lat", 1), ("lon", 2)), reach_cells, True)
    lat_first = lax.axis_index("lat") * lat_rows
    lon_first = lax.axis_index("lon") * lon_cols
    ext_col = lon_first - reach_cells + jnp.arange(ext_cols, dtype=jnp.int32)
    wrap_col = ext_col % lon_total
    mask_cols = jnp.take(key_mask, wrap_col, axis=1)
    mark_cols = wrap_col % 4 == 0
    rel_lon = (
        jnp.arange(ext_cols, dtype=jnp.int32)[None, :]
        - jnp.arange(lon_cols, dtype=jnp.int32)[:, None]
    )
    in_lon = (rel_lon >= 0) & (rel_lon < WIN)
    lon_pick = jnp.clip(rel_lon, 0, WIN - 1)
    lon_table = jnp.take(bias_table, lon_pick, axis=2).transpose(0, 2, 1, 3)
    table_pad = jnp.pad(lon_table, ((0, 0), (0, 0), (low_pad, low_pad), (0, 0)))
    query_heads = queries.reshape(lat_rows, lon_cols, head_count, HEAD_DIM)
    grad_heads = grad_attn.reshape(lat_rows, lon_cols, head_count, HEAD_DIM)

    def block_step(state_pair, block_index):
        grad_pair, table_acc = state_pair
        local_first = block_index * row_block
        top_row = lat_first + local_first
        key_first = jnp.clip(top_row - reach_cells, 0, lat_total - key_span)
        key_local = key_first - (lat_first - reach_cells)
        query_rows = top_row + jnp.arange(row_block, dtype=jnp.int32)
        window_first = jnp.clip(query_rows - reach_cells, 0, lat_total - WIN)
        key_glob = key_first + jnp.arange(key_span, dtype=jnp.int32)
        in_lat = (key_glob[None, :] >= window_first[:, None]) & (
            key_glob[None, :] < window_first[:, None] + WIN
        )
        mask_rows = lax.dynamic_slice_in_dim(mask_cols, key_first, key_span, 0)
        valid_keys = (mask_rows == 1) | (key_glob % 4 == 0)[:, None] & mark_cols[None, :]
        allowed = in_lat[:, None, :, None] & in_lon[None, :, None, :] & valid_keys[None, None, :, :]
        allowed = allowed.reshape(block_rows, block_keys)
        shifts = key_first - query_rows + (WIN - 1) + low_pad
        bias_parts = [
            lax.dynamic_slice_in_dim(table_pad, shifts[row_pos], key_span, 2)
            for row_pos in range(row_block)
        ]
        bias_rows = jnp.stack(bias_parts, axis=1).reshape(head_count, block_rows, block_keys)
        query_block = lax.dynamic_slice_in_dim(query_heads, local_first, row_block, 0).reshape(
            block_rows, head_count, HEAD_DIM
        )
        grad_block = lax.dynamic_slice_in_dim(grad_heads, local_first, row_block, 0).reshape(
            block_rows, head_count, HEAD_DIM
        )
        pair_block = lax.dynamic_slice_in_dim(extended, key_local, key_span, 1).reshape(
            2, block_keys, head_count, HEAD_DIM
        )
        key_block = pair_block[0]
        value_block = pair_block[1]
        scores = (
            score_scale
            * jnp.einsum("qhd,khd->hqk", query_block, key_block, preferred_element_type=jnp.float32)
            + bias_rows
        )
        scores = jnp.where(allowed[None], scores, -1e30)
        row_max = jnp.max(scores, axis=2, keepdims=True)
        weights_exp = jnp.exp(scores - row_max)
        prob_rows = weights_exp / jnp.sum(weights_exp, axis=2, keepdims=True)
        grad_prob = jnp.einsum(
            "qhd,khd->hqk", grad_block, value_block, preferred_element_type=jnp.float32
        )
        row_delta = jnp.sum(prob_rows * grad_prob, axis=2, keepdims=True)
        dscore = prob_rows * (grad_prob - row_delta)
        score_grid = dscore.reshape(head_count, row_block, lon_cols, key_span, ext_cols)
        score_grid = score_grid.transpose(0, 1, 3, 2, 4).reshape(
            head_count, row_block, key_span, lon_cols * ext_cols
        )
        for row_pos in range(row_block):
            prior_sum = lax.dynamic_slice_in_dim(table_acc, shifts[row_pos], key_span, 1)
            table_acc = lax.dynamic_update_slice_in_dim(
                table_acc, prior_sum + score_grid[:, row_pos], shifts[row_pos], 1
            )
        dscore_low = dscore.astype(jnp.bfloat16)
        prob_low = prob_rows.astype(jnp.bfloat16)
        grad_query = (
            score_scale
            * jnp.einsum("hqk,khd->qhd", dscore_low, key_block, preferred_element_type=jnp.float32)
        ).astype(jnp.bfloat16)
        key_part = score_scale * jnp.einsum(
            "hqk,qhd->khd", dscore_low, query_block, preferred_element_type=jnp.float32
        )
        value_part = jnp.einsum(
            "hqk,qhd->khd", prob_low, grad_block, preferred_element_type=jnp.float32
        )
        new_part = jnp.stack([key_part, value_part]).reshape(2, key_span, ext_cols, chan_width)
        prior_pair = lax.dynamic_slice_in_dim(grad_pair, key_local, key_span, 1)
        grad_pair = lax.dynamic_update_slice_in_dim(grad_pair, prior_pair + new_part, key_local, 1)
        return ((grad_pair, table_acc), grad_query)

    zero_pair = jnp.zeros((2, ext_rows, ext_cols, chan_width), jnp.float32)
    zero_table = jnp.zeros(
        (head_count, offset_rows + 2 * low_pad, lon_cols * ext_cols), jnp.float32
    )
    (grad_pair, table_acc), query_blocks = lax.scan(
        block_step, (zero_pair, zero_table), jnp.arange(block_count, dtype=jnp.int32)
    )
    grad_queries = query_blocks.reshape(lat_rows, lon_cols, chan_width)
    table_core = table_acc[:, low_pad : low_pad + offset_rows].reshape(
        head_count, offset_rows, lon_cols, ext_cols
    )
    col_take = (
        jnp.arange(lon_cols, dtype=jnp.int32)[:, None] + jnp.arange(WIN, dtype=jnp.int32)[None, :]
    )
    col_take = jnp.broadcast_to(
        col_take[None, None, :, :], (head_count, offset_rows, lon_cols, WIN)
    )
    table_local = jnp.sum(jnp.take_along_axis(table_core, col_take, axis=3), axis=2)
    grad_table = lax.psum(table_local, ("lat", "lon"))
    folded = fold_lat(fold_lon(grad_pair, lon_cols), lat_rows)
    grad_keys = folded[0].astype(jnp.bfloat16)
    grad_values = folded[1].astype(jnp.bfloat16)
    saved_out = attn_out.reshape(tokens, chan_width)
    slab_part = grad_cols
    grad_wout = lax.psum_scatter(
        jnp.dot(slab_part, saved_out, preferred_element_type=jnp.float32),
        ("lat", "lon"),
        scatter_dimension=0,
        tiled=True,
    )
    return (grad_queries, grad_keys, grad_values, grad_wout, grad_table)


def solution(mesh):
    return jax.shard_map(
        local,
        mesh=mesh,
        in_specs=(
            P("lat", "lon", "chan"),
            P("lat", "lon", "chan"),
            P("lat", "lon", "chan"),
            P("lat", "lon", "chan"),
            P("lat", "lon", "chan"),
            P(("lat", "lon"), "chan"),
            P("chan", None, None),
            P(),
        ),
        out_specs=(
            P("lat", "lon", "chan"),
            P("lat", "lon", "chan"),
            P("lat", "lon", "chan"),
            P(("lat", "lon"), "chan"),
            P("chan", None, None),
        ),
        check_vma=False,
    )
```

profile of v0, /device:TPU:240, one launch (start us, length us, event | category | flops | bytes accessed | tf_op | source)
XLA Modules:
  0.0 933.4 jit_solution(14924076082434811027)
XLA Ops:
  7.2 1.8 copy.63
  9.8 26.9 %all-gather.3.cloned.1.call-done = bf16[16,8,5120]{2,0,1:T(8,128)(2,1)} async-done(((bf16[16,8,1280]{2,0,1:T(8,128)(2,1)}), bf16[16,8,5120]{2,0,1:T(8,128)(2,1)}) %all-gather.3.cloned.1.call-update) | async-done | bytes 1310736 | tf_op jit(solution)/shard_map/all_gather | solution.py:79
  36.7 7.9 convolution_bitcast_fusion.1
  44.7 0.9 copy-done.9
  45.8 1.7 collective-permute-start.1
  49.0 1.0 collective-permute-done
  51.5 4.6 collective-permute-start.3
  56.1 1.4 gather_fusion.1
  58.2 0.9 pad.20.clone
  59.1 11.4 %collective-permute-done.3 = bf16[2,28,6,640]{3,0,2,1:T(2,128)(2,1)S(1)} collective-permute-done((bf16[2,28,6,640]{3,0,2,1:T(2,128)(2,1)S(1)}, bf16[2,28,6,640]{3,0,2,1:T(2,128)(2,1)S(1)}, u32[]{:S(2)}, u32[]{:S(2)}) %collective-permute-start.3) | collective-permute-done | bytes 430112 | tf_op jit(solution)/shard_map/ppermute | solution.py:18
  70.6 10.3 %collective-permute-done.2 = bf16[2,28,6,640]{3,0,2,1:T(2,128)(2,1)S(1)} collective-permute-done((bf16[2,28,6,640]{3,0,2,1:T(2,128)(2,1)S(1)}, bf16[2,28,6,640]{3,0,2,1:T(2,128)(2,1)S(1)}, u32[]{:S(2)}, u32[]{:S(2)}) %collective-permute-start.2) | collective-permute-done | bytes 430112 | tf_op jit(solution)/shard_map/ppermute | solution.py:17
  80.9 2.1 pad_maximum_fusion.1
  83.0 156.4 %all-gather.5.cloned.1.call-done = bf16[5120,640]{1,0:T(8,128)(2,1)} async-done(((bf16[80,640]{1,0:T(8,128)(2,1)}), bf16[5120,640]{1,0:T(8,128)(2,1)}) %all-gather.5.cloned.1.call-update) | async-done | bytes 6553616 | tf_op jit(solution)/shard_map/all_gather | solution.py:84
  239.4 4.6 fusion.42
  244.0 1.9 broadcast_in_dim.94
  245.9 117.0 %while.18 = (s32[]{:T(128)}, f32[2,28,20,640]{3,2,1,0:T(8,128)}, f32[5,31,160]{2,1,0:T(8,128)S(1)}, bf16[4,32,5,128]{3,1,2,0:T(8,128)(2,1)}, s32[4]{0:T(128)S(1)...) while((s32[]{:T(128)}, f32[2,28,20,640]{3,2,1,0:T(8,128)}, ...), condition=%wide.region_4.5_spmd.clone, body=%wide.region_0.0_spmd.clone.sunk | while | flops 67648624 | bytes 32509632 | solution.py:184
  257.6 1.3 constant_dynamic-slice_fusion.7
  259.8 1.9 dynamic-slice_bitcast_fusion.5
  265.9 1.2 stack.66
  268.0 1.2 stack.67
  272.1 3.0 fusion.106
  286.8 1.3 constant_dynamic-slice_fusion.7
  289.0 1.9 dynamic-slice_bitcast_fusion.5
  295.2 1.2 stack.66
  297.2 1.2 stack.67
  301.4 3.0 fusion.106
  316.0 1.3 constant_dynamic-slice_fusion.7
  318.3 1.9 dynamic-slice_bitcast_fusion.5
  324.4 1.2 stack.66
  326.4 1.2 stack.67
  330.6 3.1 fusion.106
  345.3 1.3 constant_dynamic-slice_fusion.7
  347.5 1.9 dynamic-slice_bitcast_fusion.5
  353.6 1.2 stack.66
  355.7 1.2 stack.67
  359.8 3.1 fusion.106
  363.0 2.2 convert.16
  365.3 1.1 copy.70
  366.5 1.1 copy.71
  367.6 2.0 collective-permute-start.4
  370.2 0.9 reshape.332
  371.3 155.3 %gather_fusion.2 = f32[13000]{0:T(1024)S(1)} fusion(f32[5,25,8,20]{3,2,1,0:T(8,128)S(1)} %reshape.333, s32[13000]{0:T(1024)S(1)} %reshape.350), kind=kCustom, calls=%fused_computation.2 | custom fusion | bytes 312000 | tf_op jit(solution)/shard_map/jit(take_along_axis)/gather | solution.py:197
  527.0 1.1 copy.73
  528.1 1.1 copy.72
  529.9 2.3 fusion.59
  532.3 2.1 collective-permute-start.6
  534.3 4.4 collective-permute-start.7
  539.0 386.1 %psum.7 = f32[5,25,13]{2,1,0:T(8,128)S(1)} all-reduce(f32[5,25,13]{2,1,0:T(8,128)S(1)} %select_reduce_fusion), channel_id=1, replica_groups=mesh['lat'=8,'lon'=8,'chan'=4] {'lat','lon'}, use_global_device_ids=true, to_apply=%region_7.8 | all-reduce | flops 1625 | bytes 13000 | tf_op jit(solution)/shard_map/psum | solution.py:198
  (281 shorter events, 57.6 us)
Async XLA Ops:
  7.2 29.5 %copy-start = (bf16[16,8,640]{2,1,0:T(8,128)(2,1)S(1)}, bf16[16,8,640]{2,1,0:T(8,128)(2,1)}, u32[]{:S(2)}) copy-start(bf16[16,8,640]{2,1,0:T(8,128)(2,1)} %param.13) | copy-start | bytes 491524
  7.2 29.5 %all-gather.3.cloned.1.call-start = ((), (), s32[]{:S(2)}) async-start(), calls=%async_computation.1 | async-start | bytes 1638400 | tf_op jit(solution)/shard_map/all_gather | solution.py:79
  9.0 230.4 %all-gather.5.cloned.1.call-start = ((), (), s32[]{:S(2)}) async-start(), calls=%async_computation.2 | async-start | bytes 6656000 | tf_op jit(solution)/shard_map/all_gather | solution.py:84
  9.8 917.1 %reduce-scatter.2.cloned.1.call-start = ((), (), s32[]{:S(2)}) async-start(), calls=%async_computation.3 | async-start | bytes 13312000 | tf_op jit(solution)/shard_map/reduce_scatter | solution.py:204
  44.6 0.9 copy-start.9
  44.6 1.0 copy-start.10
  44.6 3.0 copy-start.8
  45.7 4.4 collective-permute-start
  45.8 4.8 collective-permute-start.1
  50.6 5.5 copy-start.1
  51.5 19.0 %collective-permute-start.3 = (bf16[2,28,6,640]{3,0,2,1:T(2,128)(2,1)S(1)}, bf16[2,28,6,640]{3,0,2,1:T(2,128)(2,1)S(1)}, u32[]{:S(2)}, u32[]{:S(2)}) collective-permute-start(bf16[2,28,6,640]{3,0,2,1:T(2,128)(2,1)S(1)} %copy.59), channel_id=1, source_target_pairs={{4,0},{8,4},{12,8},{16,12},{20,16},{24,20},{28,24},{0,28},{5,1},{9... | collective-permute-start | bytes 1290248 | tf_op jit(solution)/shard_map/ppermute | solution.py:18
  56.1 24.7 %collective-permute-start.2 = (bf16[2,28,6,640]{3,0,2,1:T(2,128)(2,1)S(1)}, bf16[2,28,6,640]{3,0,2,1:T(2,128)(2,1)S(1)}, u32[]{:S(2)}, u32[]{:S(2)}) collective-permute-start(bf16[2,28,6,640]{3,0,2,1:T(2,128)(2,1)S(1)} %copy.58), channel_id=1, source_target_pairs={{0,4},{4,8},{8,12},{12,16},{16,20},{20,24},{24,28},{28,0},{1,5},{5... | collective-permute-start | bytes 1290248 | tf_op jit(solution)/shard_map/ppermute | solution.py:17
  80.9 158.5 %copy-start.11 = (bf16[16,8,5120]{2,0,1:T(8,128)(2,1)S(1)}, bf16[16,8,5120]{2,0,1:T(8,128)(2,1)}, u32[]{:S(2)}) copy-start(bf16[16,8,5120]{2,0,1:T(8,128)(2,1)} %all-gather.3.cloned.1.call-done) | copy-start | bytes 3932164
  245.9 13.4 %copy-start.12 = (bf16[16,8,5,128]{3,1,2,0:T(8,128)(2,1)}, bf16[16,8,5,128]{3,1,2,0:T(8,128)(2,1)S(1)}, u32[]{:S(2)}) copy-start(bf16[16,8,5,128]{3,1,2,0:T(8,128)(2,1)S(1)} %get-tuple-element.541) | copy-start | bytes 491524 | tf_op jit(solution)/shard_map/while
  270.5 1.5 copy-start.2
  270.9 1.3 copy-start.3
  272.1 3.0 copy-start.13
  275.2 13.4 %copy-start.12 = (bf16[16,8,5,128]{3,1,2,0:T(8,128)(2,1)}, bf16[16,8,5,128]{3,1,2,0:T(8,128)(2,1)S(1)}, u32[]{:S(2)}) copy-start(bf16[16,8,5,128]{3,1,2,0:T(8,128)(2,1)S(1)} %get-tuple-element.541) | copy-start | bytes 491524 | tf_op jit(solution)/shard_map/while
  299.7 1.5 copy-start.2
  300.1 1.3 copy-start.3
  301.4 3.0 copy-start.13
  304.4 13.4 %copy-start.12 = (bf16[16,8,5,128]{3,1,2,0:T(8,128)(2,1)}, bf16[16,8,5,128]{3,1,2,0:T(8,128)(2,1)S(1)}, u32[]{:S(2)}) copy-start(bf16[16,8,5,128]{3,1,2,0:T(8,128)(2,1)S(1)} %get-tuple-element.541) | copy-start | bytes 491524 | tf_op jit(solution)/shard_map/while
  328.9 1.5 copy-start.2
  329.3 1.3 copy-start.3
  330.6 3.1 copy-start.13
  333.6 13.4 %copy-start.12 = (bf16[16,8,5,128]{3,1,2,0:T(8,128)(2,1)}, bf16[16,8,5,128]{3,1,2,0:T(8,128)(2,1)S(1)}, u32[]{:S(2)}) copy-start(bf16[16,8,5,128]{3,1,2,0:T(8,128)(2,1)S(1)} %get-tuple-element.541) | copy-start | bytes 491524 | tf_op jit(solution)/shard_map/while
  358.2 1.5 copy-start.2
  358.6 1.3 copy-start.3
  359.8 3.1 copy-start.13
  365.3 4.3 copy-start.4
  365.3 4.3 copy-start.6
  365.3 4.7 copy-start.14
  367.6 159.4 %collective-permute-start.5 = (bf16[2,28,6,640]{3,0,2,1:T(2,128)(2,1)}, bf16[2,28,6,640]{3,0,2,1:T(2,128)(2,1)}, u32[]{:S(2)}, u32[]{:S(2)}) collective-permute-start(bf16[2,28,6,640]{3,0,2,1:T(2,128)(2,1)} %copy.71), channel_id=1, source_target_pairs={{4,0},{8,4},{12,8},{16,12},{20,16},{24,20},{28,24},{0,28},{5,1},{9... | collective-permute-start | bytes 1290248 | tf_op jit(solution)/shard_map/ppermute | solution.py:18
  367.6 160.5 %collective-permute-start.4 = (bf16[2,28,6,640]{3,0,2,1:T(2,128)(2,1)}, bf16[2,28,6,640]{3,0,2,1:T(2,128)(2,1)}, u32[]{:S(2)}, u32[]{:S(2)}) collective-permute-start(bf16[2,28,6,640]{3,0,2,1:T(2,128)(2,1)} %copy.70), channel_id=1, source_target_pairs={{0,4},{4,8},{8,12},{12,16},{16,20},{20,24},{24,28},{28,0},{1,5},{5... | collective-permute-start | bytes 1290248 | tf_op jit(solution)/shard_map/ppermute | solution.py:17
  369.6 1.7 copy-start.19
  369.6 1.7 copy-start.15
  369.6 1.7 copy-start.17
  526.6 2.6 copy-start.5
  526.6 2.6 copy-start.7
  529.2 0.7 copy-start.21
  529.9 8.9 copy-start.16
  529.9 8.9 copy-start.18
  529.9 8.9 copy-start.20
  532.2 393.8 %copy-start.22 = (pred[16]{0:T(512)(128)(4,1)S(1)}, pred[16]{0:T(512)(128)(4,1)}, u32[]{:S(2)}) copy-start(pred[16]{0:T(512)(128)(4,1)} %constant.227.clone.1) | copy-start | bytes 52
  532.3 393.6 %collective-permute-start.6 = (bf16[2,6,8,640]{3,2,1,0:T(8,128)(2,1)S(1)}, bf16[2,6,8,640]{3,2,1,0:T(8,128)(2,1)S(1)}, u32[]{:S(2)}, u32[]{:S(2)}) collective-permute-start(bf16[2,6,8,640]{3,2,1,0:T(8,128)(2,1)S(1)} %get-tuple-element.361), channel_id=1, source_target_pairs={{0,32},{32,64},{64,96},{96,128},{128,160},{160,192},{192,224},{1,3... | collective-permute-start | bytes 368648 | tf_op jit(solution)/shard_map/ppermute | solution.py:17
  534.3 391.5 %collective-permute-start.7 = (bf16[2,6,8,640]{3,2,1,0:T(8,128)(2,1)S(1)}, bf16[2,6,8,640]{3,2,1,0:T(8,128)(2,1)S(1)}, u32[]{:S(2)}, u32[]{:S(2)}) collective-permute-start(bf16[2,6,8,640]{3,2,1,0:T(8,128)(2,1)S(1)} %get-tuple-element.362), channel_id=1, source_target_pairs={{32,0},{64,32},{96,64},{128,96},{160,128},{192,160},{224,192},{33,... | collective-permute-start | bytes 368648 | tf_op jit(solution)/shard_map/ppermute | solution.py:18
Sparse Core Ops, SparseCore 0:
  9.8 26.8 all-gather.2
  38.5 200.8 all-gather.4
  242.6 461.3 reduce-scatter.1
where the time goes:
time: 935 us; the launch traced here: 933 us
  blocking collectives  386 us (41%)
  local copies, waits for them, and re-layouts  227 us (24%)
  waiting for transfers between devices  207 us (22%)
  loops' own time  33.7 us (4%)
  other arithmetic  28.7 us (3%)
  matrix products  21.7 us (2%)
  starting transfers between devices  15.1 us (2%)
  between operations  14.2 us (2%)
    psum x1, blocking collectives, local(): grad_table = lax.psum(table_local, ('lat', 'lon'))  386 us
    all_gather x1, waiting for transfers between devices, local(): lax.all_gather(w_out, ('lat', 'lon'), axis=0, tiled=True)  156 us
    gather x3, local copies, waits for them, and re-layouts, local(): jnp.take_along_axis(table_core, col_take, axis=3)  156 us
    another operation x1, loops' own time, local(): lax.scan(block_step, (zero_pair, zero_table), jnp.arange(block_count, dty...  33.7 us
    all_gather x1, waiting for transfers between devices, local(): lax.all_gather(grad_out, 'chan', axis=2, tiled=True).reshape(tokens, -1)  26.9 us
  transfers between devices with their start and end apart: 11, of which 6 were waited for; matrix products, arithmetic and copies ran while one was open for 29% of the time, Pallas kernels for 0%

commit v1 on v0

--- a/solution.py
+++ b/solution.py
@@ -81,7 +81,12 @@
     slab_part = grad_cols
     grad_attn = lax.dot_general(
         slab_part,
-        lax.all_gather(w_out, ("lat", "lon"), axis=0, tiled=True),
+        jnp.concatenate(
+            lax.all_to_all(
+                jnp.stack([w_out] * lax.axis_size(("lat", "lon"))), ("lat", "lon"), 0, 0
+            ),
+            axis=0,
+        ),
         contract_lead,
         preferred_element_type=jnp.float32,
     ).astype(jnp.bfloat16)

time: 935 us -> 1020 us (1.091)
  starting transfers between devices: 15.1 us -> 69.5 us
  blocking collectives: 386 us -> 360 us
  local copies, waits for them, and re-layouts: 227 us -> 244 us
  waiting for transfers between devices: 207 us -> 223 us
  other arithmetic: 28.7 us -> 43.3 us
    ppermute x4, waiting for transfers between devices: 11.3 us -> 193 us  [extended_2(): before = lax.ppermute(last, axis, up)]
    all_gather x1 -> x0, waiting for transfers between devices: 156 us -> none  [local(): lax.all_gather(w_out, ('lat', 'lon'), axis=0, tiled=True)]
    ppermute x4, starting transfers between devices: 10.8 us -> 57.9 us  [extended_2(): after = lax.ppermute(leading, axis, down)]
    psum x1, blocking collectives: 386 us -> 360 us  [local(): grad_table = lax.psum(table_local, ('lat', 'lon'))]
    dynamic_update_slice x16, local copies, waits for them, and re-layouts: 3.93 us -> 25.7 us  [block_step(): lax.dynamic_update_slice_in_dim(table_acc, prior_sum + score_grid[:, row_...]
    add x16, other arithmetic: 0.35 us -> 14.7 us  [block_step(): prior_sum + score_grid[:, row_pos]]
    ppermute x4, waiting for transfers between devices: 11.9 us -> 0.01 us  [extended_2(): after = lax.ppermute(leading, axis, down)]
  transfers between devices with their start and end apart: 11 -> 11, of which waited for: 6 -> 3; matrix products, arithmetic and copies ran while one was open for 29% -> 30% of each run, Pallas kernels for 0% -> 0%
where the time goes in v1:
time: 1020 us; the launch traced here: 1010 us
  blocking collectives  360 us (35%)
  local copies, waits for them, and re-layouts  244 us (24%)
  waiting for transfers between devices  223 us (22%)
  starting transfers between devices  69.5 us (7%)
  other arithmetic  43.3 us (4%)
  loops' own time  33.3 us (3%)
  matrix products  25.8 us (3%)
  between operations  14.5 us (1%)
    psum x1, blocking collectives, local(): grad_table = lax.psum(table_local, ('lat', 'lon'))  360 us
    ppermute x4, waiting for transfers between devices, extended_2(): before = lax.ppermute(last, axis, up)  193 us
    gather x3, local copies, waits for them, and re-layouts, local(): jnp.take_along_axis(table_core, col_take, axis=3)  156 us
    ppermute x4, starting transfers between devices, extended_2(): after = lax.ppermute(leading, axis, down)  57.9 us
    another operation x1, loops' own time, local(): lax.scan(block_step, (zero_pair, zero_table), jnp.arange(block_count, dty...  33.3 us
    all_gather x1, waiting for transfers between devices, local(): lax.all_gather(grad_out, 'chan', axis=2, tiled=True).reshape(tokens, -1)  29.7 us
    dynamic_update_slice x16, local copies, waits for them, and re-layouts, block_step(): lax.dynamic_update_slice_in_dim(table_acc, prior_sum + score_grid[:, row_...  25.7 us
  transfers between devices with their start and end apart: 11, of which 3 were waited for; matrix products, arithmetic and copies ran while one was open for 30% of the time, Pallas kernels for 0%

profile of v1, /device:TPU:240, one launch (start us, length us, event | category | flops | bytes accessed | tf_op | source)
XLA Modules:
  0.0 1014.2 jit_solution(1577536986394125391)
XLA Ops:
  7.2 4.2 stack.47
  11.4 9.4 all-to-all-start
  21.7 29.7 %all-gather.2.cloned.1.call-done = bf16[16,8,5120]{2,0,1:T(8,128)(2,1)} async-done(((bf16[16,8,1280]{2,0,1:T(8,128)(2,1)}), bf16[16,8,5120]{2,0,1:T(8,128)(2,1)}) %all-gather.2.cloned.1.call-update) | async-done | bytes 1310736 | tf_op jit(solution)/shard_map/all_gather | solution.py:79
  51.4 7.9 convolution_bitcast_fusion.1
  60.5 1.7 collective-permute-start.1
  63.7 161.5 %collective-permute-done = bf16[2,6,8,640]{3,2,1,0:T(8,128)(2,1)S(1)} collective-permute-done((bf16[2,6,8,640]{3,2,1,0:T(8,128)(2,1)S(1)}, bf16[2,6,8,640]{3,2,1,0:T(8,128)(2,1)S(1)}, u32[]{:S(2)}, u32[]{:S(2)}) %collective-permute-start) | collective-permute-done | bytes 122912 | tf_op jit(solution)/shard_map/ppermute | solution.py:17
  226.3 44.5 %collective-permute-start.3 = (bf16[2,28,6,640]{3,0,2,1:T(2,128)(2,1)S(1)}, bf16[2,28,6,640]{3,0,2,1:T(2,128)(2,1)}, u32[]{:S(2)}, u32[]{:S(2)}) collective-permute-start(bf16[2,28,6,640]{3,0,2,1:T(2,128)(2,1)S(1)} %copy.59), channel_id=1, source_target_pairs={{4,0},{8,4},{12,8},{16,12},{20,16},{24,20},{28,24},{0,28},{5,1},{9... | collective-permute-start | bytes 1290248 | tf_op jit(solution)/shard_map/ppermute | solution.py:18
  270.8 1.4 gather_fusion.1
  272.9 31.8 %collective-permute-done.2 = bf16[2,28,6,640]{3,0,2,1:T(2,128)(2,1)S(1)} collective-permute-done((bf16[2,28,6,640]{3,0,2,1:T(2,128)(2,1)S(1)}, bf16[2,28,6,640]{3,0,2,1:T(2,128)(2,1)S(1)}, u32[]{:S(2)}, u32[]{:S(2)}) %collective-permute-start.2) | collective-permute-done | bytes 430112 | tf_op jit(solution)/shard_map/ppermute | solution.py:17
  305.9 2.0 pad_maximum_fusion.1
  308.0 5.1 fusion.42
  313.1 1.9 broadcast_in_dim.94
  315.7 147.0 %while.18 = (s32[]{:T(128)}, f32[2,28,20,640]{3,2,1,0:T(8,128)}, f32[5,31,160]{2,1,0:T(8,128)}, bf16[4,32,5,128]{3,1,2,0:T(8,128)(2,1)}, s32[4]{0:T(128)S(1)}, /...) while((s32[]{:T(128)}, f32[2,28,20,640]{3,2,1,0:T(8,128)}, ...), condition=%wide.region_4.5_spmd.clone, body=%wide.region_0.0_spmd.clone.sunk | while | flops 67648624 | bytes 28716212 | solution.py:189
  334.9 1.6 dynamic_update_slice.59
  337.4 1.6 dynamic_update_slice.60
  339.9 1.6 dynamic_update_slice.61
  342.5 1.6 dynamic_update_slice.62
  345.2 1.4 convolution_bitcast_fusion.3
  346.6 1.7 copy.122
  348.5 3.1 fusion.106
  371.6 1.6 dynamic_update_slice.59
  374.1 1.6 dynamic_update_slice.60
  376.7 1.6 dynamic_update_slice.61
  379.2 1.6 dynamic_update_slice.62
  381.9 1.4 convolution_bitcast_fusion.3
  383.4 1.7 copy.122
  385.3 3.1 fusion.106
  408.4 1.6 dynamic_update_slice.59
  410.9 1.6 dynamic_update_slice.60
  413.4 1.6 dynamic_update_slice.61
  415.9 1.6 dynamic_update_slice.62
  418.6 1.4 convolution_bitcast_fusion.3
  420.1 1.7 copy.122
  422.0 3.1 fusion.106
  445.1 1.6 dynamic_update_slice.59
  447.6 1.6 dynamic_update_slice.60
  450.1 1.6 dynamic_update_slice.61
  452.7 1.6 dynamic_update_slice.62
  455.4 1.4 convolution_bitcast_fusion.3
  456.8 1.7 copy.122
  458.7 3.1 fusion.106
  462.7 2.2 convert.16
  467.3 8.0 collective-permute-start.5
  477.5 155.3 %gather_fusion.2 = f32[13000]{0:T(1024)S(1)} fusion(f32[5,25,8,20]{3,2,1,0:T(8,128)S(1)} %reshape.339, s32[13000]{0:T(1024)S(1)} %reshape.356), kind=kCustom, calls=%fused_computation.2 | custom fusion | bytes 312000 | tf_op jit(solution)/shard_map/jit(take_along_axis)/gather | solution.py:202
  636.1 2.4 fusion.59
  638.5 1.9 collective-permute-start.6
  640.4 3.6 collective-permute-start.7
  644.3 360.3 %psum.7 = f32[5,25,13]{2,1,0:T(8,128)S(1)} all-reduce(f32[5,25,13]{2,1,0:T(8,128)S(1)} %select_reduce_fusion), channel_id=1, replica_groups=mesh['lat'=8,'lon'=8,'chan'=4] {'lat','lon'}, use_global_device_ids=true, to_apply=%region_7.8 | all-reduce | flops 1625 | bytes 13000 | tf_op jit(solution)/shard_map/psum | solution.py:203
  (285 shorter events, 80.8 us)
Async XLA Ops:
  7.2 44.2 %copy-start = (bf16[16,8,640]{2,1,0:T(8,128)(2,1)S(1)}, bf16[16,8,640]{2,1,0:T(8,128)(2,1)}, u32[]{:S(2)}) copy-start(bf16[16,8,640]{2,1,0:T(8,128)(2,1)} %param.13) | copy-start | bytes 491524
  11.4 9.5 copy-start.15
  11.4 296.6 %all-to-all-start = ((bf16[64,80,640]{2,1,0:T(8,128)(2,1)}), bf16[64,80,640]{2,1,0:T(8,128)(2,1)}, u32[]{:S(2)}, u32[]{:S(2)}) async-start(bf16[64,80,640]{2,1,0:T(8,128)(2,1)} %stack.47), calls=%async_computation | async-start | bytes 13107200 | tf_op jit(solution)/shard_map/all_to_all | solution.py:85
  20.8 30.6 %all-gather.2.cloned.1.call-start = ((), (), s32[]{:S(2)}) async-start(), calls=%async_computation.2 | async-start | bytes 1638400 | tf_op jit(solution)/shard_map/all_gather | solution.py:79
  21.7 985.7 %reduce-scatter.2.cloned.1.call-start = ((), (), s32[]{:S(2)}) async-start(), calls=%async_computation.3 | async-start | bytes 13312000 | tf_op jit(solution)/shard_map/reduce_scatter | solution.py:209
  59.4 0.9 copy-start.12
  59.4 1.0 copy-start.13
  59.4 2.9 copy-start.11
  60.4 164.8 %collective-permute-start = (bf16[2,6,8,640]{3,2,1,0:T(8,128)(2,1)S(1)}, bf16[2,6,8,640]{3,2,1,0:T(8,128)(2,1)S(1)}, u32[]{:S(2)}, u32[]{:S(2)}) collective-permute-start(bf16[2,6,8,640]{3,2,1,0:T(8,128)(2,1)S(1)} %get-tuple-element.367), channel_id=1, source_target_pairs={{0,32},{32,64},{64,96},{96,128},{128,160},{160,192},{192,224},{224... | collective-permute-start | bytes 368648 | tf_op jit(solution)/shard_map/ppermute | solution.py:17
  60.5 164.8 %collective-permute-start.1 = (bf16[2,6,8,640]{3,2,1,0:T(8,128)(2,1)S(1)}, bf16[2,6,8,640]{3,2,1,0:T(8,128)(2,1)S(1)}, u32[]{:S(2)}, u32[]{:S(2)}) collective-permute-start(bf16[2,6,8,640]{3,2,1,0:T(8,128)(2,1)S(1)} %get-tuple-element.368), channel_id=1, source_target_pairs={{32,0},{64,32},{96,64},{128,96},{160,128},{192,160},{224,192},{0,2... | collective-permute-start | bytes 368648 | tf_op jit(solution)/shard_map/ppermute | solution.py:18
  225.3 45.5 %copy-start.2 = (f32[5,25,13]{1,2,0:T(8,128)S(1)}, f32[5,25,13]{1,2,0:T(8,128)}, u32[]{:S(2)}) copy-start(f32[5,25,13]{1,2,0:T(8,128)} %param.16) | copy-start | bytes 19504
  225.9 78.9 %collective-permute-start.2 = (bf16[2,28,6,640]{3,0,2,1:T(2,128)(2,1)S(1)}, bf16[2,28,6,640]{3,0,2,1:T(2,128)(2,1)S(1)}, u32[]{:S(2)}, u32[]{:S(2)}) collective-permute-start(bf16[2,28,6,640]{3,0,2,1:T(2,128)(2,1)S(1)} %copy.58), channel_id=1, source_target_pairs={{0,4},{4,8},{8,12},{12,16},{16,20},{20,24},{24,28},{28,0},{1,5},{5... | collective-permute-start | bytes 1290248 | tf_op jit(solution)/shard_map/ppermute | solution.py:17
  226.3 78.5 %collective-permute-start.3 = (bf16[2,28,6,640]{3,0,2,1:T(2,128)(2,1)S(1)}, bf16[2,28,6,640]{3,0,2,1:T(2,128)(2,1)}, u32[]{:S(2)}, u32[]{:S(2)}) collective-permute-start(bf16[2,28,6,640]{3,0,2,1:T(2,128)(2,1)S(1)} %copy.59), channel_id=1, source_target_pairs={{4,0},{8,4},{12,8},{16,12},{20,16},{24,20},{28,24},{0,28},{5,1},{9... | collective-permute-start | bytes 1290248 | tf_op jit(solution)/shard_map/ppermute | solution.py:18
  305.9 2.0 copy-start.14
  315.7 9.7 copy-start.5
  329.3 2.9 copy-start.3
  348.5 3.1 copy-start.4
  348.5 3.9 copy-start.6
  352.5 9.7 copy-start.5
  366.0 2.9 copy-start.3
  385.2 3.1 copy-start.4
  385.3 3.9 copy-start.6
  389.2 9.7 copy-start.5
  402.7 2.9 copy-start.3
  422.0 3.1 copy-start.4
  422.0 4.0 copy-start.6
  425.9 9.7 copy-start.5
  439.5 2.9 copy-start.3
  458.7 3.2 copy-start.4
  458.7 4.0 copy-start.6
  465.0 10.4 %copy-start.7 = (bf16[2,28,6,640]{3,2,1,0:T(8,128)(2,1)}, bf16[2,28,6,640]{3,2,1,0:T(8,128)(2,1)S(1)}, u32[]{:S(2)}) copy-start(bf16[2,28,6,640]{3,2,1,0:T(8,128)(2,1)S(1)} %get-tuple-element.359) | copy-start | bytes 1290244
  465.1 10.4 %copy-start.9 = (bf16[2,28,6,640]{3,2,1,0:T(8,128)(2,1)}, bf16[2,28,6,640]{3,2,1,0:T(8,128)(2,1)S(1)}, u32[]{:S(2)}) copy-start(bf16[2,28,6,640]{3,2,1,0:T(8,128)(2,1)S(1)} %get-tuple-element.360) | copy-start | bytes 1290244
  466.2 167.0 %collective-permute-start.4 = (bf16[2,28,6,640]{3,0,2,1:T(2,128)(2,1)}, bf16[2,28,6,640]{3,0,2,1:T(2,128)(2,1)}, u32[]{:S(2)}, u32[]{:S(2)}) collective-permute-start(bf16[2,28,6,640]{3,0,2,1:T(2,128)(2,1)} %copy.70), channel_id=1, source_target_pairs={{0,4},{4,8},{8,12},{12,16},{16,20},{20,24},{24,28},{28,0},{1,5},{5... | collective-permute-start | bytes 1290248 | tf_op jit(solution)/shard_map/ppermute | solution.py:17
  467.3 167.0 %collective-permute-start.5 = (bf16[2,28,6,640]{3,0,2,1:T(2,128)(2,1)}, bf16[2,28,6,640]{3,0,2,1:T(2,128)(2,1)}, u32[]{:S(2)}, u32[]{:S(2)}) collective-permute-start(bf16[2,28,6,640]{3,0,2,1:T(2,128)(2,1)} %copy.71), channel_id=1, source_target_pairs={{4,0},{8,4},{12,8},{16,12},{20,16},{24,20},{28,24},{0,28},{5,1},{9... | collective-permute-start | bytes 1290248 | tf_op jit(solution)/shard_map/ppermute | solution.py:18
  475.4 0.5 copy-start.21
  475.4 0.6 copy-start.17
  475.4 0.6 copy-start.19
  632.8 2.6 copy-start.8
  632.8 2.6 copy-start.10
  635.4 0.7 copy-start.23
  636.1 8.0 copy-start.18
  636.1 8.0 copy-start.20
  636.1 8.0 copy-start.22
  636.1 369.3 %copy-start.16 = (bf16[4,32,5,128]{3,1,2,0:T(8,128)(2,1)S(1)}, bf16[4,32,5,128]{3,1,2,0:T(8,128)(2,1)}, u32[]{:S(2)}) copy-start(bf16[4,32,5,128]{3,1,2,0:T(8,128)(2,1)} %get-tuple-element.218) | copy-start | bytes 491524
  638.5 367.8 %collective-permute-start.6 = (bf16[2,6,8,640]{3,2,1,0:T(8,128)(2,1)S(1)}, bf16[2,6,8,640]{3,2,1,0:T(8,128)(2,1)S(1)}, u32[]{:S(2)}, u32[]{:S(2)}) collective-permute-start(bf16[2,6,8,640]{3,2,1,0:T(8,128)(2,1)S(1)} %get-tuple-element.361), channel_id=1, source_target_pairs={{0,32},{32,64},{64,96},{96,128},{128,160},{160,192},{192,224},{1,3... | collective-permute-start | bytes 368648 | tf_op jit(solution)/shard_map/ppermute | solution.py:17
  640.4 365.9 %collective-permute-start.7 = (bf16[2,6,8,640]{3,2,1,0:T(8,128)(2,1)S(1)}, bf16[2,6,8,640]{3,2,1,0:T(8,128)(2,1)S(1)}, u32[]{:S(2)}, u32[]{:S(2)}) collective-permute-start(bf16[2,6,8,640]{3,2,1,0:T(8,128)(2,1)S(1)} %get-tuple-element.362), channel_id=1, source_target_pairs={{32,0},{64,32},{96,64},{128,96},{160,128},{192,160},{224,192},{33,... | collective-permute-start | bytes 368648 | tf_op jit(solution)/shard_map/ppermute | solution.py:18
  644.3 362.2 %copy-start.24 = (pred[16]{0:T(512)(128)(4,1)S(1)}, pred[16]{0:T(512)(128)(4,1)}, u32[]{:S(2)}) copy-start(pred[16]{0:T(512)(128)(4,1)} %constant.227.clone.1) | copy-start | bytes 52
  1006.3 1.0 copy-start.1
Sparse Core Ops, SparseCore 0:
  23.4 27.9 all-gather.1
  59.5 554.8 reduce-scatter.1
